TPU v7x, 256 devices: a whole 4x4x8 slice. The times are simulated.
256 devices in a mesh: upd: 8 (over x, core), col: 32 (over z, y).
Axes of the slice: x: 4, y: 4, z: 8, core: 2. Of those that a mesh axis runs over, the one named last changes fastest.
Arguments:
- panel: bfloat16 [32, 8, 1024, 1024], P('col', None, 'upd'), may hold values from -6 to 6
- diag_tiles: bfloat16 [32, 1024, 1024], P('col', 'upd'), may hold values from -6 to 6
- dinv: bfloat16 [32, 1024, 1024], P('col'), may hold values from -1 to 1, as said below
- u_fac: bfloat16 [32, 8, 8, 96, 1024], P('col', None, 'upd'), may hold values from -1.1953125 to 1.1953125
- v_fac: bfloat16 [32, 8, 8, 96, 1024], P('col', None, 'upd'), may hold values from -1.1953125 to 1.1953125
- ranks: int32 [32, 8, 8], P('col', None, 'upd'), may hold values from 1 to 96, as said below
- sketch: bfloat16 [32, 64, 1024], P('col'), may hold values from -6 to 6
Outputs:
- panel_out: bfloat16 [32, 8, 1024, 1024], P('col', None, 'upd')
- diag_out: float32 [32, 1024, 1024], P('col', 'upd')
Inputs may be any that keep to these rules, and one draw needn't show every extreme that they name: `ranks`: in every panel tile at least two of the 8 pieces have rank 96. `dinv`: each block is lower triangular with a positive diagonal.
All inputs are finite; a program needn't handle non-finite values.
Results may differ from a plain program's by a relative error of at most 0.014.
Values may be sent and summed in bfloat16 or wider, within the bound.
No kernel may reach another device: no remote copies, remote signals or barrier semaphores. Data moves between devices by JAX's collectives and lax.ppermute only.
A program may use at most 64 MiB of HBM per device.

v0:
```python
import jax
import jax.numpy as jnp
from jax import lax
from jax.sharding import PartitionSpec as P


def in_blocks(array, dim, peers):
    dims = array.shape
    parts = array.reshape(*dims[:dim], peers, dims[dim] // peers, *dims[dim + 1 :])
    return jnp.moveaxis(parts, dim, 0)


def sum_at_owner(array, axis, dim):
    parts = in_blocks(array, dim, lax.axis_size(axis))
    arrived = lax.all_to_all(parts, axis, split_axis=0, concat_axis=0, tiled=True)
    return arrived.astype(jnp.float32).sum(axis=0)


def copy_for_each(array, axis):
    peers = lax.axis_size(axis)
    return lax.all_to_all(
        jnp.broadcast_to(array[None], (peers, *array.shape)), axis, 0, 0, tiled=True
    )


def laid_out(parts, dim):
    parts = jnp.moveaxis(parts, 0, dim)
    dims = parts.shape
    return parts.reshape(*dims[:dim], dims[dim] * dims[dim + 1], *dims[dim + 2 :])


def gathered_copies(array, axis, dim):
    parts = copy_for_each(array, axis)
    return laid_out(parts, dim)


def padded_to(lines, peers):
    spare = -len(lines) % peers
    return jnp.pad(lines, [(0, spare)] + [(0, 0)] * (lines.ndim - 1))


def sum_by_parts(array, axis):
    lines = array.reshape(-1, *array.shape[1:][-1:])
    own = lax.psum_scatter(
        padded_to(lines, lax.axis_size(axis)), axis, scatter_dimension=0, tiled=True
    )
    whole = lax.all_gather(own, axis).reshape(-1, *lines.shape[1:])
    return lax.slice_in_dim(whole, 0, len(lines)).reshape(array.shape)


def shifted(block, axis, distance):
    devices = range(lax.axis_size(axis))
    route = [(i - distance, i) for i in devices if i - distance in devices]
    return lax.ppermute(block, axis, route)


def orthonormal(summed):
    gram = jnp.einsum("kb,lb->kl", summed, summed, precision=lax.Precision.HIGHEST)
    chol = jnp.linalg.cholesky(gram)
    return jax.scipy.linalg.solve_triangular(chol, summed, lower=True).astype(jnp.bfloat16)


def local(panel, diag_tiles, dinv, u_fac, v_fac, ranks, sketch):
    left_factor = u_fac[0, :, 0]
    right_factor = v_fac[0, :, 0]
    slots = lax.broadcasted_iota(jnp.int32, (1, left_factor.shape[1], 1), 1)
    keep = slots < ranks[0, :, 0][:, None, None]
    random_probe = jnp.einsum(
        "jef,yf->jey", right_factor, sketch[0], preferred_element_type=jnp.float32
    )
    random_probe = jnp.where(keep, random_probe, 0.0).astype(jnp.bfloat16)
    range_component = jnp.einsum(
        "zgj,zgp->zpj", left_factor, random_probe, preferred_element_type=jnp.float32
    )
    share = sum_at_owner(range_component.astype(jnp.bfloat16), "upd", 0)
    range_basis = gathered_copies(jax.vmap(orthonormal)(share), "upd", 0)
    coefficient_matrix = jnp.einsum(
        "wxj,wuj->wxu", left_factor, range_basis, preferred_element_type=jnp.float32
    )
    coefficient_matrix = jnp.where(keep, coefficient_matrix, 0.0).astype(jnp.bfloat16)
    cross_term_part = jnp.einsum(
        "zgj,zgp->zpj", right_factor, coefficient_matrix, preferred_element_type=jnp.float32
    )
    cross_term = (
        sum_by_parts(cross_term_part.astype(jnp.bfloat16), "upd")
        .astype(jnp.float32)
        .astype(jnp.bfloat16)
    )
    rows_dev = panel.shape[2]
    first_row = lax.axis_index("upd") * rows_dev
    range_basis_rows = lax.dynamic_slice_in_dim(range_basis, first_row, rows_dev, 2)
    approximation = jnp.einsum(
        "fei,fej->fij", range_basis_rows, cross_term, preferred_element_type=jnp.float32
    )
    updated_tile = (panel[0].astype(jnp.float32) - approximation).astype(jnp.bfloat16)
    lowrank_factor = jnp.einsum(
        "vxn,en->vxe", updated_tile, dinv[0], preferred_element_type=jnp.float32
    ).astype(jnp.bfloat16)
    band = lowrank_factor.shape[0]
    received = jnp.stack(
        [shifted(lowrank_factor[offset - 1], "col", offset) for offset in range(1, band + 1)]
    )
    columns = lax.all_to_all(received, "upd", split_axis=2, concat_axis=1, tiled=True)
    total = sum_at_owner(
        (-jnp.einsum("mrc,mnc->rn", columns, columns, preferred_element_type=jnp.float32)).astype(
            jnp.bfloat16
        ),
        "upd",
        0,
    )
    diag_out = (diag_tiles[0].astype(jnp.float32) + total)[None]
    return (lowrank_factor[None], diag_out)


def solution(mesh):
    in_specs = (
        P("col", None, "upd", None),
        P("col", "upd", None),
        P("col", None, None),
        P("col", None, "upd", None, None),
        P("col", None, "upd", None, None),
        P("col", None, "upd"),
        P("col", None, None),
    )
    out_specs = (P("col", None, "upd", None), P("col", "upd", None))
    return jax.shard_map(local, mesh=mesh, in_specs=in_specs, out_specs=out_specs, check_vma=False)
```

profile of v0, /device:TPU:160, one launch (start us, length us, event | category | flops | bytes accessed | tf_op | source)
XLA Modules:
  0.0 297.2 jit_solution(5002424032824517877)
XLA Ops:
  7.2 0.0 reduce-scatter.2.cloned.1.call-start
  7.2 0.9 iota_compare_fusion.2
  8.1 2.9 fusion.21
  11.0 20.1 %all_to_all.33 = bf16[8,1,64,1024]{3,2,1,0:T(8,128)(2,1)S(1)} all-to-all(bf16[8,1,64,1024]{3,2,1,0:T(8,128)(2,1)S(1)} %fusion.21), channel_id=1, replica_groups=mesh['upd'=8,'col'=32] {'upd'}, dimensions={0} | all-to-all | bytes 2097152 | tf_op jit(solution)/shard_map/all_to_all | solution.py:15
  31.1 0.2 convert_reduce_fusion.1
  31.3 0.4 fusion.59
  31.6 0.1 copy.14
  31.7 5.8 %custom-call.8 = f32[1,64,64]{2,1,0:T(8,128)S(1)} custom-call(f32[1,64,64]{2,1,0:T(8,128)S(1)} %fusion.53), custom_call_target="Cholesky" | custom-call | tf_op jit(solution)/shard_map/vmap(jit(cholesky))/cholesky | solution.py:59
  37.6 0.6 compare_reduce_fusion
  38.3 0.7 fusion.52
  38.9 4.9 %custom-call.9 = f32[1,1,64,64]{2,3,1,0:T(8,128)S(1)} custom-call(f32[1,1,64,64]{3,2,1,0:T(8,128)S(1)} %fusion.52), custom_call_target="InvertDiagBlocksLowerTriangular" | custom-call | tf_op jit(solution)/shard_map/vmap(jit(_solve_triangular))/triangular_solve | solution.py:60
  43.8 0.4 convolution_convert_fusion
  44.3 0.1 broadcast_in_dim.36
  44.4 18.4 %all_to_all.34 = bf16[8,1,64,1024]{3,2,1,0:T(8,128)(2,1)S(1)} all-to-all(bf16[8,1,64,1024]{3,2,1,0:T(8,128)(2,1)S(1)} %broadcast_in_dim.36), channel_id=1, replica_groups=mesh['upd'=8,'col'=32] {'upd'}, dimensions={0} | all-to-all | bytes 2097152 | tf_op jit(solution)/shard_map/all_to_all | solution.py:21
  62.8 3.8 %fusion.15 = bf16[8,64,1024]{2,1,0:T(8,128)(2,1)} fusion(bf16[1,8,1,96,1024]{4,3,2,1,0:T(8,128)(2,1)} %param.11, bf16[1,8,1,96,1024]{4,3,2,1,0:T(8,128)(2,1)} %param.10, bf16[8,1,64,1024]{3,2,1,0:T(8,128)(2,1)S(1)} %all_to_all.34, pred[8,96]{1,0:T(8,128)(4,1)S(1)} %iota_compare_fusion.2), kind=kOutput, calls=%fused_computation.17 | convolution fusion | flops 201949184 | bytes 5243648 | tf_op jit(solution)/shard_map/zgj,zgp->zpj/dot_general | solution.py:81
  66.6 0.0 reduce-scatter.2.cloned.1.call-update
  66.6 0.0 all-gather.3.cloned.1.call-start
  66.7 34.1 %reduce-scatter.2.cloned.1.call-done = bf16[64,1024]{1,0:T(8,128)(2,1)} async-done(((bf16[512,1024]{1,0:T(8,128)(2,1)}), bf16[64,1024]{1,0:T(8,128)(2,1)}) %reduce-scatter.2.cloned.1.call-update) | async-done | bytes 131088 | tf_op jit(solution)/shard_map/reduce_scatter | solution.py:44
  100.8 26.5 %all-gather.3.cloned.1.call-done = bf16[512,1024]{1,0:T(8,128)(2,1)} async-done(((bf16[64,1024]{1,0:T(8,128)(2,1)}), bf16[512,1024]{1,0:T(8,128)(2,1)}) %all-gather.3.cloned.1.call-update) | async-done | bytes 1048592 | tf_op jit(solution)/shard_map/all_gather | solution.py:47
  127.3 6.2 %fusion.4 = bf16[8,128,1024]{2,1,0:T(8,128)(2,1)} fusion(bf16[1,1024,1024]{2,1,0:T(8,128)(2,1)S(1)} %copy-done, bf16[8,64,1024]{2,1,0:T(8,128)(2,1)} %bitcast.126, bf16[1,8,128,1024]{3,2,1,0:T(8,128)(2,1)} %param.7, bf16[8,1,64,1024]{3,2,1,0:T(8,128)(2,1)S(1)} %all_to_all.34, s32[]{:T(128)S(6)} %select_n.17), kind=kOutput, calls=%fused_computation.8 | convolution fusion | flops 2285895680 | bytes 7471108 | tf_op jit(solution)/shard_map/vxn,en->vxe/dot_general | solution.py:96
  133.6 1.7 slice_bitcast_fusion
  135.3 3.4 %collective-permute-start = (bf16[128,1024]{1,0:T(8,128)(2,1)S(1)}, bf16[128,1024]{1,0:T(8,128)(2,1)S(1)}, u32[]{:S(2)}, u32[]{:S(2)}) collective-permute-start(bf16[128,1024]{1,0:T(8,128)(2,1)S(1)} %get-tuple-element.9), channel_id=1, source_target_pairs={{0,1},{1,2},{2,3},{3,4},{4,5},{5,6},{6,7},{7,8},{8,9},{9,10},{10,1... | collective-permute-start | bytes 786440 | tf_op jit(solution)/shard_map/ppermute | solution.py:54
  138.7 4.6 %collective-permute-start.1 = (bf16[128,1024]{1,0:T(8,128)(2,1)S(1)}, bf16[128,1024]{1,0:T(8,128)(2,1)S(1)}, u32[]{:S(2)}, u32[]{:S(2)}) collective-permute-start(bf16[128,1024]{1,0:T(8,128)(2,1)S(1)} %get-tuple-element.8), channel_id=1, source_target_pairs={{0,2},{1,3},{2,4},{3,5},{4,6},{5,7},{6,8},{7,9},{8,10},{9,11},{10,... | collective-permute-start | bytes 786440 | tf_op jit(solution)/shard_map/ppermute | solution.py:54
  143.3 2.7 collective-permute-start.7
  146.0 2.2 collective-permute-start.6
  148.2 1.9 collective-permute-start.5
  150.1 0.1 collective-permute-done
  150.2 4.9 %collective-permute-start.2 = (bf16[128,1024]{1,0:T(8,128)(2,1)S(1)}, bf16[128,1024]{1,0:T(8,128)(2,1)S(1)}, u32[]{:S(2)}, u32[]{:S(2)}) collective-permute-start(bf16[128,1024]{1,0:T(8,128)(2,1)S(1)} %get-tuple-element.7), channel_id=1, source_target_pairs={{0,3},{1,4},{2,5},{3,6},{4,7},{5,8},{6,9},{7,10},{8,11},{9,12},{10... | collective-permute-start | bytes 786440 | tf_op jit(solution)/shard_map/ppermute | solution.py:54
  155.1 0.7 bitcast_dynamic-update-slice_fusion.7
  155.8 2.6 collective-permute-start.3
  158.4 0.7 bitcast_dynamic-update-slice_fusion.6
  159.1 22.9 %collective-permute-done.2 = bf16[128,1024]{1,0:T(8,128)(2,1)S(1)} collective-permute-done((bf16[128,1024]{1,0:T(8,128)(2,1)S(1)}, bf16[128,1024]{1,0:T(8,128)(2,1)S(1)}, u32[]{:S(2)}, u32[]{:S(2)}) %collective-permute-start.2) | collective-permute-done | bytes 262176 | tf_op jit(solution)/shard_map/ppermute | solution.py:54
  182.1 13.4 %collective-permute-start.4 = (bf16[128,1024]{1,0:T(8,128)(2,1)S(1)}, bf16[128,1024]{1,0:T(8,128)(2,1)S(1)}, u32[]{:S(2)}, u32[]{:S(2)}) collective-permute-start(bf16[128,1024]{1,0:T(8,128)(2,1)S(1)} %get-tuple-element.5), channel_id=1, source_target_pairs={{0,5},{1,6},{2,7},{3,8},{4,9},{5,10},{6,11},{7,12},{8,13},{9,14},{... | collective-permute-start | bytes 786440 | tf_op jit(solution)/shard_map/ppermute | solution.py:54
  195.5 0.7 bitcast_dynamic-update-slice_fusion.5
  196.2 0.7 bitcast_dynamic-update-slice_fusion.4
  197.0 14.6 %collective-permute-done.4 = bf16[128,1024]{1,0:T(8,128)(2,1)S(1)} collective-permute-done((bf16[128,1024]{1,0:T(8,128)(2,1)S(1)}, bf16[128,1024]{1,0:T(8,128)(2,1)S(1)}, u32[]{:S(2)}, u32[]{:S(2)}) %collective-permute-start.4) | collective-permute-done | bytes 262176 | tf_op jit(solution)/shard_map/ppermute | solution.py:54
  211.6 0.7 bitcast_dynamic-update-slice_fusion.3
  212.3 0.7 bitcast_dynamic-update-slice_fusion.2
  213.1 0.7 bitcast_dynamic-update-slice_fusion.1
  213.8 0.7 bitcast_dynamic-update-slice_fusion
  214.5 4.2 %copy.15 = bf16[8,128,1024]{1,0,2:T(8,128)(2,1)} copy(bf16[8,128,1024]{2,1,0:T(8,128)(2,1)} %bitcast_dynamic-update-slice_fusion) | data formatting | bytes 4194304 | tf_op jit(solution)/shard_map/stack | solution.py:100
  218.7 31.6 %all_to_all.35 = bf16[8,128,1024]{1,0,2:T(8,128)(2,1)} all-to-all(bf16[8,128,1024]{1,0,2:T(8,128)(2,1)} %copy.15), channel_id=1, replica_groups=mesh['upd'=8,'col'=32] {'upd'}, dimensions={2} | all-to-all | bytes 4194304 | tf_op jit(solution)/shard_map/all_to_all | solution.py:103
  250.2 4.1 %copy.16 = bf16[8,128,8,128]{3,1,2,0:T(8,128)(2,1)} copy(bf16[8,128,8,128]{1,0,3,2:T(8,128)(2,1)} %bitcast.120) | data formatting | bytes 4194304 | tf_op jit(solution)/shard_map/all_to_all | solution.py:103
  254.4 4.6 %fusion.1 = bf16[1024,1024]{1,0:T(8,128)(2,1)S(1)} fusion(bf16[8,1024,128]{2,1,0:T(8,128)(2,1)} %bitcast.123), kind=kOutput, calls=%fused_computation.3 | convolution fusion | flops 2149580800 | bytes 4194304 | tf_op jit(solution)/shard_map/mrc,mnc->rn/dot_general | solution.py:105
  258.9 29.7 %all_to_all.36 = bf16[8,128,1024]{2,1,0:T(8,128)(2,1)S(1)} all-to-all(bf16[8,128,1024]{2,1,0:T(8,128)(2,1)S(1)} %bitcast.124), channel_id=1, replica_groups=mesh['upd'=8,'col'=32] {'upd'}, dimensions={0} | all-to-all | bytes 4194304 | tf_op jit(solution)/shard_map/all_to_all | solution.py:15
  288.6 0.4 convert_reduce_fusion
  289.0 0.6 copy-done.1
  289.6 0.8 bitcast_add_fusion
  (11 shorter events, 0.1 us)
Async XLA Ops:
  7.2 120.2 %copy-start = (bf16[1,1024,1024]{2,1,0:T(8,128)(2,1)S(1)}, bf16[1,1024,1024]{2,1,0:T(8,128)(2,1)}, u32[]{:S(2)}) copy-start(bf16[1,1024,1024]{2,1,0:T(8,128)(2,1)} %param.9) | copy-start | bytes 6291460
  7.2 93.6 %reduce-scatter.2.cloned.1.call-start = ((), (), s32[]{:S(2)}) async-start(), calls=%async_computation.5 | async-start | bytes 1179648 | tf_op jit(solution)/shard_map/reduce_scatter | solution.py:44
  66.6 60.7 %all-gather.3.cloned.1.call-start = ((), (), s32[]{:S(2)}) async-start(), calls=%async_computation.6 | async-start | bytes 1179648 | tf_op jit(solution)/shard_map/all_gather | solution.py:47
  135.3 14.9 %collective-permute-start = (bf16[128,1024]{1,0:T(8,128)(2,1)S(1)}, bf16[128,1024]{1,0:T(8,128)(2,1)S(1)}, u32[]{:S(2)}, u32[]{:S(2)}) collective-permute-start(bf16[128,1024]{1,0:T(8,128)(2,1)S(1)} %get-tuple-element.9), channel_id=1, source_target_pairs={{0,1},{1,2},{2,3},{3,4},{4,5},{5,6},{6,7},{7,8},{8,9},{9,10},{10,1... | collective-permute-start | bytes 786440 | tf_op jit(solution)/shard_map/ppermute | solution.py:54
  138.7 17.1 %collective-permute-start.1 = (bf16[128,1024]{1,0:T(8,128)(2,1)S(1)}, bf16[128,1024]{1,0:T(8,128)(2,1)S(1)}, u32[]{:S(2)}, u32[]{:S(2)}) collective-permute-start(bf16[128,1024]{1,0:T(8,128)(2,1)S(1)} %get-tuple-element.8), channel_id=1, source_target_pairs={{0,2},{1,3},{2,4},{3,5},{4,6},{5,7},{6,8},{7,9},{8,10},{9,11},{10,... | collective-permute-start | bytes 786440 | tf_op jit(solution)/shard_map/ppermute | solution.py:54
  143.3 70.4 %collective-permute-start.7 = (bf16[128,1024]{1,0:T(8,128)(2,1)S(1)}, bf16[128,1024]{1,0:T(8,128)(2,1)S(1)}, u32[]{:S(2)}, u32[]{:S(2)}) collective-permute-start(bf16[128,1024]{1,0:T(8,128)(2,1)S(1)} %get-tuple-element.2), channel_id=1, source_target_pairs={{0,8},{1,9},{2,10},{3,11},{4,12},{5,13},{6,14},{7,15},{8,16},{9,17... | collective-permute-start | bytes 786440 | tf_op jit(solution)/shard_map/ppermute | solution.py:54
  146.0 67.1 %collective-permute-start.6 = (bf16[128,1024]{1,0:T(8,128)(2,1)S(1)}, bf16[128,1024]{1,0:T(8,128)(2,1)S(1)}, u32[]{:S(2)}, u32[]{:S(2)}) collective-permute-start(bf16[128,1024]{1,0:T(8,128)(2,1)S(1)} %get-tuple-element.3), channel_id=1, source_target_pairs={{0,7},{1,8},{2,9},{3,10},{4,11},{5,12},{6,13},{7,14},{8,15},{9,16}... | collective-permute-start | bytes 786440 | tf_op jit(solution)/shard_map/ppermute | solution.py:54
  148.2 64.1 %collective-permute-start.5 = (bf16[128,1024]{1,0:T(8,128)(2,1)S(1)}, bf16[128,1024]{1,0:T(8,128)(2,1)S(1)}, u32[]{:S(2)}, u32[]{:S(2)}) collective-permute-start(bf16[128,1024]{1,0:T(8,128)(2,1)S(1)} %get-tuple-element.4), channel_id=1, source_target_pairs={{0,6},{1,7},{2,8},{3,9},{4,10},{5,11},{6,12},{7,13},{8,14},{9,15},... | collective-permute-start | bytes 786440 | tf_op jit(solution)/shard_map/ppermute | solution.py:54
  150.2 31.8 %collective-permute-start.2 = (bf16[128,1024]{1,0:T(8,128)(2,1)S(1)}, bf16[128,1024]{1,0:T(8,128)(2,1)S(1)}, u32[]{:S(2)}, u32[]{:S(2)}) collective-permute-start(bf16[128,1024]{1,0:T(8,128)(2,1)S(1)} %get-tuple-element.7), channel_id=1, source_target_pairs={{0,3},{1,4},{2,5},{3,6},{4,7},{5,8},{6,9},{7,10},{8,11},{9,12},{10... | collective-permute-start | bytes 786440 | tf_op jit(solution)/shard_map/ppermute | solution.py:54
  155.8 40.4 %collective-permute-start.3 = (bf16[128,1024]{1,0:T(8,128)(2,1)S(1)}, bf16[128,1024]{1,0:T(8,128)(2,1)S(1)}, u32[]{:S(2)}, u32[]{:S(2)}) collective-permute-start(bf16[128,1024]{1,0:T(8,128)(2,1)S(1)} %get-tuple-element.6), channel_id=1, source_target_pairs={{0,4},{1,5},{2,6},{3,7},{4,8},{5,9},{6,10},{7,11},{8,12},{9,13},{1... | collective-permute-start | bytes 786440 | tf_op jit(solution)/shard_map/ppermute | solution.py:54
  182.1 29.5 %collective-permute-start.4 = (bf16[128,1024]{1,0:T(8,128)(2,1)S(1)}, bf16[128,1024]{1,0:T(8,128)(2,1)S(1)}, u32[]{:S(2)}, u32[]{:S(2)}) collective-permute-start(bf16[128,1024]{1,0:T(8,128)(2,1)S(1)} %get-tuple-element.5), channel_id=1, source_target_pairs={{0,5},{1,6},{2,7},{3,8},{4,9},{5,10},{6,11},{7,12},{8,13},{9,14},{... | collective-permute-start | bytes 786440 | tf_op jit(solution)/shard_map/ppermute | solution.py:54
  288.6 1.0 copy-start.1
Sparse Core Ops, SparseCore 0:
  66.8 33.9 reduce-scatter.1
  102.7 24.6 all-gather.2
where the time goes:
time: 298 us; the launch traced here: 297 us
  blocking collectives  99.7 us (33%)
  waiting for transfers between devices  98.3 us (33%)
  starting transfers between devices  35.7 us (12%)
  matrix products  18.4 us (6%)
  local copies, waits for them, and re-layouts  16.6 us (6%)
  other arithmetic  14.3 us (5%)
  between operations  14.2 us (5%)
    all_to_all x2, blocking collectives, sum_at_owner(): lax.all_to_all(parts, axis, split_axis=0, concat_axis=0, tiled=True)  49.7 us
    ppermute x8, waiting for transfers between devices, shifted(): return lax.ppermute(block, axis, route)  37.7 us
    ppermute x8, starting transfers between devices, shifted(): return lax.ppermute(block, axis, route)  35.6 us
    reduce_scatter x1, waiting for transfers between devices, sum_by_parts(): lax.psum_scatter(padded_to(lines, lax.axis_size(axis)), axis, scatter_dim...  34.1 us
    all_to_all x1, blocking collectives, local(): lax.all_to_all(received, 'upd', split_axis=2, concat_axis=1, tiled=True)  31.6 us
    all_gather x1, waiting for transfers between devices, sum_by_parts(): whole = lax.all_gather(own, axis).reshape(-1, *lines.shape[1:])  26.5 us
    all_to_all x1, blocking collectives, copy_for_each(): lax.all_to_all(jnp.broadcast_to(array[None], (peers, *array.shape)), axis...  18.4 us
    another operation x3, other arithmetic, orthonormal(): chol = jnp.linalg.cholesky(gram)  6.52 us
  transfers between devices with their start and end apart: 10, of which 5 were waited for; matrix products, arithmetic and copies ran while one was open for 2% of the time, Pallas kernels for 0%

commit v1 on v0

--- a/solution.py
+++ b/solution.py
@@ -2,6 +2,15 @@
 import jax.numpy as jnp
 from jax import lax
 from jax.sharding import PartitionSpec as P
+
+
+def arrange_column(here_x):
+    return jnp.concatenate(
+        lax.all_to_all(
+            jnp.stack(jnp.split(here_x, lax.axis_size("upd"), axis=2), axis=0), "upd", 0, 0
+        ),
+        axis=1,
+    )
 
 
 def in_blocks(array, dim, peers):
@@ -100,7 +109,7 @@
     received = jnp.stack(
         [shifted(lowrank_factor[offset - 1], "col", offset) for offset in range(1, band + 1)]
     )
-    columns = lax.all_to_all(received, "upd", split_axis=2, concat_axis=1, tiled=True)
+    columns = arrange_column(received)
     total = sum_at_owner(
         (-jnp.einsum("mrc,mnc->rn", columns, columns, preferred_element_type=jnp.float32)).astype(
             jnp.bfloat16

time: 298 us -> 284 us (0.953)
  local copies, waits for them, and re-layouts: 16.6 us -> 3.61 us
    another operation x2 -> x1, local copies, waits for them, and re-layouts: 4.88 us -> 0.02 us  [local(): jnp.stack([shifted(lowrank_factor[offset - 1], 'col', offset) for offset...]
    unnamed x11 -> x18, local copies, waits for them, and re-layouts: 5.71 us -> 1.34 us
    all_to_all x1 -> x0, local copies, waits for them, and re-layouts: 4.13 us -> none  [local(): lax.all_to_all(received, 'upd', split_axis=2, concat_axis=1, tiled=True)]
  transfers between devices with their start and end apart: 10 -> 10, of which waited for: 5 -> 5; matrix products, arithmetic and copies ran while one was open for 2% -> 0% of each run, Pallas kernels for 0% -> 0%
where the time goes in v1:
time: 284 us; the launch traced here: 283 us
  waiting for transfers between devices  101 us (36%)
  blocking collectives  98 us (35%)
  starting transfers between devices  35.7 us (13%)
  matrix products  16.2 us (6%)
  between operations  14.4 us (5%)
  other arithmetic  14.3 us (5%)
  local copies, waits for them, and re-layouts  3.61 us (1%)
    all_to_all x2, blocking collectives, sum_at_owner(): lax.all_to_all(parts, axis, split_axis=0, concat_axis=0, tiled=True)  49.7 us
    ppermute x8, waiting for transfers between devices, shifted(): return lax.ppermute(block, axis, route)  40.5 us
    ppermute x8, starting transfers between devices, shifted(): return lax.ppermute(block, axis, route)  35.7 us
    reduce_scatter x1, waiting for transfers between devices, sum_by_parts(): lax.psum_scatter(padded_to(lines, lax.axis_size(axis)), axis, scatter_dim...  34.1 us
    all_to_all x1, blocking collectives, arrange_column(): lax.all_to_all(jnp.stack(jnp.split(here_x, lax.axis_size('upd'), axis=2),...  29.9 us
    all_gather x1, waiting for transfers between devices, sum_by_parts(): whole = lax.all_gather(own, axis).reshape(-1, *lines.shape[1:])  26.5 us
    all_to_all x1, blocking collectives, copy_for_each(): lax.all_to_all(jnp.broadcast_to(array[None], (peers, *array.shape)), axis...  18.4 us
    another operation x3, other arithmetic, orthonormal(): chol = jnp.linalg.cholesky(gram)  6.52 us
  transfers between devices with their start and end apart: 10, of which 5 were waited for; matrix products, arithmetic and copies ran while one was open for 0% of the time, Pallas kernels for 0%

profile of v1, /device:TPU:160, one launch (start us, length us, event | category | flops | bytes accessed | tf_op | source)
XLA Modules:
  0.0 283.3 jit_solution(11677934313091907578)
XLA Ops:
  7.2 0.0 reduce-scatter.2.cloned.1.call-start
  7.2 0.9 iota_compare_fusion.2
  8.1 2.9 %fusion.21 = bf16[8,1,64,1024]{3,2,1,0:T(8,128)(2,1)S(1)} fusion(bf16[1,8,1,96,1024]{4,3,2,1,0:T(8,128)(2,1)} %param.10, bf16[1,8,1,96,1024]{4,3,2,1,0:T(8,128)(2,1)} %param.11, bf16[1,64,1024]{2,1,0:T(8,128)(2,1)} %param.13, pred[8,96]{1,0:T(8,128)(4,1)S(1)} %iota_compare_fusion.2), kind=kOutput, calls=%fused_computation.19 | convolution fusion | flops 201949184 | bytes 4326144 | tf_op jit(solution)/shard_map/zgj,zgp->zpj/dot_general | solution.py:81
  11.0 20.1 %all_to_all.20 = bf16[8,1,64,1024]{3,2,1,0:T(8,128)(2,1)S(1)} all-to-all(bf16[8,1,64,1024]{3,2,1,0:T(8,128)(2,1)S(1)} %fusion.21), channel_id=1, replica_groups=mesh['upd'=8,'col'=32] {'upd'}, dimensions={0} | all-to-all | bytes 2097152 | tf_op jit(solution)/shard_map/all_to_all | solution.py:24
  31.1 0.2 convert_reduce_fusion.1
  31.3 0.4 fusion.67
  31.6 0.1 copy.20
  31.7 5.8 %custom-call.8 = f32[1,64,64]{2,1,0:T(8,128)S(1)} custom-call(f32[1,64,64]{2,1,0:T(8,128)S(1)} %fusion.61), custom_call_target="Cholesky" | custom-call | tf_op jit(solution)/shard_map/vmap(jit(cholesky))/cholesky | solution.py:68
  37.6 0.6 compare_reduce_fusion
  38.3 0.7 fusion.60
  38.9 4.9 %custom-call.9 = f32[1,1,64,64]{2,3,1,0:T(8,128)S(1)} custom-call(f32[1,1,64,64]{3,2,1,0:T(8,128)S(1)} %fusion.60), custom_call_target="InvertDiagBlocksLowerTriangular" | custom-call | tf_op jit(solution)/shard_map/vmap(jit(_solve_triangular))/triangular_solve | solution.py:69
  43.8 0.4 convolution_convert_fusion
  44.3 0.1 broadcast_in_dim.36
  44.4 18.4 %all_to_all.21 = bf16[8,1,64,1024]{3,2,1,0:T(8,128)(2,1)S(1)} all-to-all(bf16[8,1,64,1024]{3,2,1,0:T(8,128)(2,1)S(1)} %broadcast_in_dim.36), channel_id=1, replica_groups=mesh['upd'=8,'col'=32] {'upd'}, dimensions={0} | all-to-all | bytes 2097152 | tf_op jit(solution)/shard_map/all_to_all | solution.py:30
  62.8 3.8 %fusion.15 = bf16[8,64,1024]{2,1,0:T(8,128)(2,1)} fusion(bf16[1,8,1,96,1024]{4,3,2,1,0:T(8,128)(2,1)} %param.11, bf16[1,8,1,96,1024]{4,3,2,1,0:T(8,128)(2,1)} %param.10, bf16[8,1,64,1024]{3,2,1,0:T(8,128)(2,1)S(1)} %all_to_all.21, pred[8,96]{1,0:T(8,128)(4,1)S(1)} %iota_compare_fusion.2), kind=kOutput, calls=%fused_computation.17 | convolution fusion | flops 201949184 | bytes 5243648 | tf_op jit(solution)/shard_map/zgj,zgp->zpj/dot_general | solution.py:90
  66.6 0.0 reduce-scatter.2.cloned.1.call-update
  66.6 0.0 all-gather.3.cloned.1.call-start
  66.7 34.1 %reduce-scatter.2.cloned.1.call-done = bf16[64,1024]{1,0:T(8,128)(2,1)} async-done(((bf16[512,1024]{1,0:T(8,128)(2,1)}), bf16[64,1024]{1,0:T(8,128)(2,1)}) %reduce-scatter.2.cloned.1.call-update) | async-done | bytes 131088 | tf_op jit(solution)/shard_map/reduce_scatter | solution.py:53
  100.8 0.0 all-gather.3.cloned.1.call-update
  100.8 26.5 %all-gather.3.cloned.1.call-done = bf16[512,1024]{1,0:T(8,128)(2,1)} async-done(((bf16[64,1024]{1,0:T(8,128)(2,1)}), bf16[512,1024]{1,0:T(8,128)(2,1)}) %all-gather.3.cloned.1.call-update) | async-done | bytes 1048592 | tf_op jit(solution)/shard_map/all_gather | solution.py:56
  127.3 6.2 %fusion.4 = bf16[8,128,1024]{2,1,0:T(8,128)(2,1)} fusion(bf16[1,1024,1024]{2,1,0:T(8,128)(2,1)S(1)} %copy-done, bf16[8,64,1024]{2,1,0:T(8,128)(2,1)} %bitcast.156, bf16[1,8,128,1024]{3,2,1,0:T(8,128)(2,1)} %param.7, bf16[8,1,64,1024]{3,2,1,0:T(8,128)(2,1)S(1)} %all_to_all.21, s32[]{:T(128)S(6)} %select_n.17), kind=kOutput, calls=%fused_computation.8 | convolution fusion | flops 2285895680 | bytes 7471108 | tf_op jit(solution)/shard_map/vxn,en->vxe/dot_general | solution.py:105
  133.6 1.7 slice_bitcast_fusion.8
  135.3 3.4 %collective-permute-start = (bf16[128,1024]{1,0:T(8,128)(2,1)S(1)}, bf16[128,1024]{1,0:T(8,128)(2,1)S(1)}, u32[]{:S(2)}, u32[]{:S(2)}) collective-permute-start(bf16[128,1024]{1,0:T(8,128)(2,1)S(1)} %get-tuple-element.9), channel_id=1, source_target_pairs={{0,1},{1,2},{2,3},{3,4},{4,5},{5,6},{6,7},{7,8},{8,9},{9,10},{10,1... | collective-permute-start | bytes 786440 | tf_op jit(solution)/shard_map/ppermute | solution.py:63
  138.7 4.6 %collective-permute-start.1 = (bf16[128,1024]{1,0:T(8,128)(2,1)S(1)}, bf16[128,1024]{1,0:T(8,128)(2,1)S(1)}, u32[]{:S(2)}, u32[]{:S(2)}) collective-permute-start(bf16[128,1024]{1,0:T(8,128)(2,1)S(1)} %get-tuple-element.8), channel_id=1, source_target_pairs={{0,2},{1,3},{2,4},{3,5},{4,6},{5,7},{6,8},{7,9},{8,10},{9,11},{10,... | collective-permute-start | bytes 786440 | tf_op jit(solution)/shard_map/ppermute | solution.py:63
  143.3 2.7 collective-permute-start.7
  146.0 2.2 collective-permute-start.6
  148.2 1.9 collective-permute-start.5
  150.1 0.1 collective-permute-done
  150.2 4.9 %collective-permute-start.2 = (bf16[128,1024]{1,0:T(8,128)(2,1)S(1)}, bf16[128,1024]{1,0:T(8,128)(2,1)S(1)}, u32[]{:S(2)}, u32[]{:S(2)}) collective-permute-start(bf16[128,1024]{1,0:T(8,128)(2,1)S(1)} %get-tuple-element.7), channel_id=1, source_target_pairs={{0,3},{1,4},{2,5},{3,6},{4,7},{5,8},{6,9},{7,10},{8,11},{9,12},{10... | collective-permute-start | bytes 786440 | tf_op jit(solution)/shard_map/ppermute | solution.py:63
  155.1 2.6 collective-permute-start.3
  157.7 24.3 %collective-permute-done.2 = bf16[128,1024]{1,0:T(8,128)(2,1)S(1)} collective-permute-done((bf16[128,1024]{1,0:T(8,128)(2,1)S(1)}, bf16[128,1024]{1,0:T(8,128)(2,1)S(1)}, u32[]{:S(2)}, u32[]{:S(2)}) %collective-permute-start.2) | collective-permute-done | bytes 262176 | tf_op jit(solution)/shard_map/ppermute | solution.py:63
  182.1 13.4 %collective-permute-start.4 = (bf16[128,1024]{1,0:T(8,128)(2,1)S(1)}, bf16[128,1024]{1,0:T(8,128)(2,1)S(1)}, u32[]{:S(2)}, u32[]{:S(2)}) collective-permute-start(bf16[128,1024]{1,0:T(8,128)(2,1)S(1)} %get-tuple-element.5), channel_id=1, source_target_pairs={{0,5},{1,6},{2,7},{3,8},{4,9},{5,10},{6,11},{7,12},{8,13},{9,14},{... | collective-permute-start | bytes 786440 | tf_op jit(solution)/shard_map/ppermute | solution.py:63
  195.6 16.0 %collective-permute-done.4 = bf16[128,1024]{1,0:T(8,128)(2,1)S(1)} collective-permute-done((bf16[128,1024]{1,0:T(8,128)(2,1)S(1)}, bf16[128,1024]{1,0:T(8,128)(2,1)S(1)}, u32[]{:S(2)}, u32[]{:S(2)}) %collective-permute-start.4) | collective-permute-done | bytes 262176 | tf_op jit(solution)/shard_map/ppermute | solution.py:63
  211.7 0.1 fusion.49
  211.8 0.1 fusion.48
  211.9 0.1 fusion.47
  212.0 0.1 fusion.46
  212.1 0.1 fusion.45
  212.2 0.1 fusion.44
  212.3 0.1 fusion.43
  212.4 0.1 fusion.42
  212.5 29.9 %all_to_all.22 = bf16[8,8,128,128]{3,2,1,0:T(8,128)(2,1)S(1)} all-to-all(bf16[8,8,128,128]{3,2,1,0:T(8,128)(2,1)S(1)} %fusion.42), channel_id=1, replica_groups=mesh['upd'=8,'col'=32] {'upd'}, dimensions={0} | all-to-all | bytes 4194304 | tf_op jit(solution)/shard_map/all_to_all | solution.py:9
  242.4 0.2 copy.21
  242.6 2.4 fusion.1
  245.0 29.7 %all_to_all.23 = bf16[8,128,1024]{2,1,0:T(8,128)(2,1)S(1)} all-to-all(bf16[8,128,1024]{2,1,0:T(8,128)(2,1)S(1)} %bitcast.154), channel_id=1, replica_groups=mesh['upd'=8,'col'=32] {'upd'}, dimensions={0} | all-to-all | bytes 4194304 | tf_op jit(solution)/shard_map/all_to_all | solution.py:24
  274.6 0.4 convert_reduce_fusion
  275.0 0.6 copy-done.1
  275.6 0.8 bitcast_add_fusion
  (18 shorter events, 0.2 us)
Async XLA Ops:
  7.2 120.2 %copy-start = (bf16[1,1024,1024]{2,1,0:T(8,128)(2,1)S(1)}, bf16[1,1024,1024]{2,1,0:T(8,128)(2,1)}, u32[]{:S(2)}) copy-start(bf16[1,1024,1024]{2,1,0:T(8,128)(2,1)} %param.9) | copy-start | bytes 6291460
  7.2 93.6 %reduce-scatter.2.cloned.1.call-start = ((), (), s32[]{:S(2)}) async-start(), calls=%async_computation.5 | async-start | bytes 1179648 | tf_op jit(solution)/shard_map/reduce_scatter | solution.py:53
  66.6 60.7 %all-gather.3.cloned.1.call-start = ((), (), s32[]{:S(2)}) async-start(), calls=%async_computation.6 | async-start | bytes 1179648 | tf_op jit(solution)/shard_map/all_gather | solution.py:56
  135.3 14.9 %collective-permute-start = (bf16[128,1024]{1,0:T(8,128)(2,1)S(1)}, bf16[128,1024]{1,0:T(8,128)(2,1)S(1)}, u32[]{:S(2)}, u32[]{:S(2)}) collective-permute-start(bf16[128,1024]{1,0:T(8,128)(2,1)S(1)} %get-tuple-element.9), channel_id=1, source_target_pairs={{0,1},{1,2},{2,3},{3,4},{4,5},{5,6},{6,7},{7,8},{8,9},{9,10},{10,1... | collective-permute-start | bytes 786440 | tf_op jit(solution)/shard_map/ppermute | solution.py:63
  138.7 16.4 %collective-permute-start.1 = (bf16[128,1024]{1,0:T(8,128)(2,1)S(1)}, bf16[128,1024]{1,0:T(8,128)(2,1)S(1)}, u32[]{:S(2)}, u32[]{:S(2)}) collective-permute-start(bf16[128,1024]{1,0:T(8,128)(2,1)S(1)} %get-tuple-element.8), channel_id=1, source_target_pairs={{0,2},{1,3},{2,4},{3,5},{4,6},{5,7},{6,8},{7,9},{8,10},{9,11},{10,... | collective-permute-start | bytes 786440 | tf_op jit(solution)/shard_map/ppermute | solution.py:63
  143.3 68.4 %collective-permute-start.7 = (bf16[128,1024]{1,0:T(8,128)(2,1)S(1)}, bf16[128,1024]{1,0:T(8,128)(2,1)S(1)}, u32[]{:S(2)}, u32[]{:S(2)}) collective-permute-start(bf16[128,1024]{1,0:T(8,128)(2,1)S(1)} %get-tuple-element.2), channel_id=1, source_target_pairs={{0,8},{1,9},{2,10},{3,11},{4,12},{5,13},{6,14},{7,15},{8,16},{9,17... | collective-permute-start | bytes 786440 | tf_op jit(solution)/shard_map/ppermute | solution.py:63
  146.0 65.7 %collective-permute-start.6 = (bf16[128,1024]{1,0:T(8,128)(2,1)S(1)}, bf16[128,1024]{1,0:T(8,128)(2,1)S(1)}, u32[]{:S(2)}, u32[]{:S(2)}) collective-permute-start(bf16[128,1024]{1,0:T(8,128)(2,1)S(1)} %get-tuple-element.3), channel_id=1, source_target_pairs={{0,7},{1,8},{2,9},{3,10},{4,11},{5,12},{6,13},{7,14},{8,15},{9,16}... | collective-permute-start | bytes 786440 | tf_op jit(solution)/shard_map/ppermute | solution.py:63
  148.2 63.4 %collective-permute-start.5 = (bf16[128,1024]{1,0:T(8,128)(2,1)S(1)}, bf16[128,1024]{1,0:T(8,128)(2,1)S(1)}, u32[]{:S(2)}, u32[]{:S(2)}) collective-permute-start(bf16[128,1024]{1,0:T(8,128)(2,1)S(1)} %get-tuple-element.4), channel_id=1, source_target_pairs={{0,6},{1,7},{2,8},{3,9},{4,10},{5,11},{6,12},{7,13},{8,14},{9,15},... | collective-permute-start | bytes 786440 | tf_op jit(solution)/shard_map/ppermute | solution.py:63
  150.2 31.8 %collective-permute-start.2 = (bf16[128,1024]{1,0:T(8,128)(2,1)S(1)}, bf16[128,1024]{1,0:T(8,128)(2,1)S(1)}, u32[]{:S(2)}, u32[]{:S(2)}) collective-permute-start(bf16[128,1024]{1,0:T(8,128)(2,1)S(1)} %get-tuple-element.7), channel_id=1, source_target_pairs={{0,3},{1,4},{2,5},{3,6},{4,7},{5,8},{6,9},{7,10},{8,11},{9,12},{10... | collective-permute-start | bytes 786440 | tf_op jit(solution)/shard_map/ppermute | solution.py:63
  155.1 40.4 %collective-permute-start.3 = (bf16[128,1024]{1,0:T(8,128)(2,1)S(1)}, bf16[128,1024]{1,0:T(8,128)(2,1)S(1)}, u32[]{:S(2)}, u32[]{:S(2)}) collective-permute-start(bf16[128,1024]{1,0:T(8,128)(2,1)S(1)} %get-tuple-element.6), channel_id=1, source_target_pairs={{0,4},{1,5},{2,6},{3,7},{4,8},{5,9},{6,10},{7,11},{8,12},{9,13},{1... | collective-permute-start | bytes 786440 | tf_op jit(solution)/shard_map/ppermute | solution.py:63
  182.1 29.5 %collective-permute-start.4 = (bf16[128,1024]{1,0:T(8,128)(2,1)S(1)}, bf16[128,1024]{1,0:T(8,128)(2,1)S(1)}, u32[]{:S(2)}, u32[]{:S(2)}) collective-permute-start(bf16[128,1024]{1,0:T(8,128)(2,1)S(1)} %get-tuple-element.5), channel_id=1, source_target_pairs={{0,5},{1,6},{2,7},{3,8},{4,9},{5,10},{6,11},{7,12},{8,13},{9,14},{... | collective-permute-start | bytes 786440 | tf_op jit(solution)/shard_map/ppermute | solution.py:63
  274.6 1.0 copy-start.1
Sparse Core Ops, SparseCore 0:
  66.8 33.9 reduce-scatter.1
  102.7 24.6 all-gather.2
